TPU v7x, 32 devices: a whole 2x2x4 slice. The times are simulated.
32 devices in a mesh: blk: 16 (over z, x, core), sub: 2 (over y).
Axes of the slice: x: 2, y: 2, z: 4, core: 2. Of those that a mesh axis runs over, the one named last changes fastest.
Arguments:
- vectors: bfloat16 [16, 131072], P('sub', 'blk')
- energies: float32 [131072], P('blk'), may hold values from 1 to 4
- tile_values: bfloat16 [16, 128, 128, 128], P('blk', 'sub'), may hold values from -0.1875 to 0.1875
- tile_rows: int32 [16, 128], P('blk', 'sub'), may hold values from 0 to 63
- tile_cols: int32 [16, 128], P('blk', 'sub'), may hold values from 0 to 63
- tile_offsets: int32 [16, 128], P('blk', 'sub'), may hold values from 0 to 2, as said below
- tile_count: int32 [16, 2], P('blk', 'sub'), may hold values from 8 to 64, as said below
Outputs:
- residual: float32 [16, 131072], P('sub', 'blk')
Inputs may be any that keep to these rules, and one draw needn't show every extreme that they name: `tile_offsets`: an offset never exceeds the row block's index b; where the offset is 0, tile_rows >= tile_cols. `tile_count`: each count is 64 divided by 1, 2, 4 or 8.
All inputs are finite; a program needn't handle non-finite values.
Results may differ from a plain program's by a relative error of at most 0.0003.
Values may be sent and summed in bfloat16 or wider, within the bound.
No kernel may reach another device: no remote copies, remote signals or barrier semaphores. Data moves between devices by JAX's collectives and lax.ppermute only.
A program may use at most 64 MiB of HBM per device.

v0:
```python
import jax
import jax.numpy as jnp
from jax import lax
from jax.sharding import PartitionSpec as P

BW = 2


def from_behind(value, axis, steps):
    count = lax.axis_size(axis)
    first, last = (max(0, -steps), min(count, count - steps))
    return lax.ppermute(value, axis, [(source, source + steps) for source in range(first, last)])


def ritz_coefficients(gram, projected):
    lower = jnp.linalg.cholesky(gram)
    half = lax.linalg.triangular_solve(lower, projected, left_side=True, lower=True)
    return lax.linalg.triangular_solve(lower, half, left_side=True, lower=True, transpose_a=True)


def tile_products(tile_vals, row_ids, col_ids, offset_ids, live, stacked, own_block):
    width, rows_dev = own_block.shape
    tile_side = tile_vals.shape[-1]
    row_tiles = rows_dev // tile_side
    depth = stacked.shape[0]
    highest = lax.Precision.HIGHEST
    grid_view = stacked.reshape(depth, width, row_tiles, tile_side)
    sources = grid_view[offset_ids, :, col_ids, :]
    direct_terms = jnp.einsum(
        "tij,tcj->tci", tile_vals, sources, preferred_element_type=jnp.float32
    )
    own_tiles = own_block.reshape(width, row_tiles, tile_side)[:, row_ids, :]
    mirror_terms = jnp.einsum(
        "tji,ctj->tci", tile_vals, own_tiles, preferred_element_type=jnp.float32
    )
    tile_range = jnp.arange(row_tiles, dtype=jnp.int32)
    row_hot = (row_ids[:, None] == tile_range[None, :]).astype(jnp.float32) * live[:, None]
    col_hot = (col_ids[:, None] == tile_range[None, :]).astype(jnp.float32) * live[:, None]
    depth_hot = (offset_ids[:, None] == jnp.arange(depth, dtype=jnp.int32)[None, :]).astype(
        jnp.float32
    )
    direct = jnp.einsum("tci,tr->cri", direct_terms, row_hot, precision=highest).reshape(
        width, rows_dev
    )
    mirror = jnp.einsum("tci,tk,tr->kcri", mirror_terms, depth_hot, col_hot, precision=highest)
    return (direct, mirror.reshape(depth, width, rows_dev))


def send_back(pieces):
    gathered_sum = pieces[0]
    for offset in range(1, BW + 1):
        gathered_sum = gathered_sum + from_behind(pieces[offset], "blk", -offset)
    return gathered_sum


def on_device(vectors, energies, tile_values, tile_rows, tile_cols, tile_offsets, tile_count):
    columns = vectors.shape[0]
    part_index = lax.axis_index("sub")
    tile_vals = tile_values[0]
    row_ids = tile_rows[0]
    col_ids = tile_cols[0]
    offset_ids = tile_offsets[0]
    live_count = tile_count[0, 0]
    slots = tile_vals.shape[0]
    whole = lax.all_gather(vectors, "sub", axis=0, tiled=True)
    lowered = [whole]
    for offset in range(1, BW + 1):
        lowered.append(from_behind(whole, "blk", offset))
    stacked = jnp.stack(lowered, 0)
    own_block = stacked[0]
    width, rows_dev = own_block.shape
    live = (jnp.arange(slots, dtype=jnp.int32) < live_count).astype(jnp.float32)
    direct, mirror = tile_products(
        tile_vals, row_ids, col_ids, offset_ids, live, stacked, own_block
    )
    mirror = mirror.at[0].add(direct)
    applied = lax.psum_scatter(send_back(mirror), "sub", scatter_dimension=0, tiled=True)
    applied = applied + energies[None, :] * vectors.astype(jnp.float32)
    highest = lax.Precision.HIGHEST
    own_wide = own_block.astype(jnp.float32)
    gram_part = jnp.dot(own_block, vectors.T, preferred_element_type=jnp.float32)
    proj_part = jnp.dot(own_wide, applied.T, precision=highest)
    empty = jnp.zeros((width, width), jnp.float32)
    gram_full = lax.dynamic_update_slice(empty, gram_part, (0, part_index * columns))
    proj_full = lax.dynamic_update_slice(empty, proj_part, (0, part_index * columns))
    gram, projected = lax.psum((gram_full, proj_full), ("blk", "sub"))
    coefficients = ritz_coefficients(gram, projected)
    mine = lax.dynamic_slice_in_dim(coefficients, part_index * columns, columns, 1)
    return applied - jnp.dot(mine.T, own_wide, precision=highest)


def solution(mesh):
    in_specs = (
        P("sub", "blk"),
        P("blk"),
        P("blk", "sub", None, None),
        P("blk", "sub"),
        P("blk", "sub"),
        P("blk", "sub"),
        P("blk", "sub"),
    )
    out_specs = P("sub", "blk")
    return jax.shard_map(
        on_device, mesh=mesh, in_specs=in_specs, out_specs=out_specs, check_vma=False
    )
```

profile of v0, /device:TPU:0, one launch (start us, length us, event | category | flops | bytes accessed | tf_op | source)
XLA Modules:
  0.0 120.7 jit_solution(16180372393465413950)
XLA Ops:
  6.5 7.5 %all_gather.3 = bf16[16,8192]{1,0:T(8,128)(2,1)S(1)} all-gather(bf16[8,8192]{1,0:T(8,128)(2,1)} %param.9), channel_id=1, replica_groups=mesh['blk'=16,'sub'=2] {'sub'}, dimensions={0}, use_global_device_ids=true | all-gather | bytes 393216 | tf_op jit(solution)/shard_map/all_gather | solution.py:65
  14.1 3.6 %collective-permute-start.1 = (bf16[16,8192]{1,0:T(8,128)(2,1)S(1)}, bf16[16,8192]{1,0:T(8,128)(2,1)S(1)}, u32[]{:S(2)}, u32[]{:S(2)}) collective-permute-start(bf16[16,8192]{1,0:T(8,128)(2,1)S(1)} %all_gather.3), channel_id=1, source_target_pairs={{0,4},{2,6},{4,8},{6,10},{8,12},{10,14},{12,16},{14,18},{16,20},{1... | collective-permute-start | bytes 786440 | tf_op jit(solution)/shard_map/ppermute | solution.py:12
  17.6 1.3 %collective-permute-start = (bf16[16,8192]{1,0:T(8,128)(2,1)S(1)}, bf16[16,8192]{1,0:T(8,128)(2,1)S(1)}, u32[]{:S(2)}, u32[]{:S(2)}) collective-permute-start(bf16[16,8192]{1,0:T(8,128)(2,1)S(1)} %all_gather.3), channel_id=1, source_target_pairs={{0,2},{2,4},{4,6},{6,8},{8,10},{10,12},{12,14},{14,16},{16,18},{18... | collective-permute-start | bytes 786440 | tf_op jit(solution)/shard_map/ppermute | solution.py:12
  19.0 0.7 fusion.30
  19.7 0.7 fusion.29
  21.6 0.7 fusion.2
  22.3 1.4 %convolution_bitcast_fusion = f32[3,16,64,128]{3,2,1,0:T(8,128)S(1)} fusion(f32[64,16,128]{2,1,0:T(8,128)S(1)} %fusion.2, f32[64,3]{0,1:T(4,128)S(1)} %fusion.29, f32[64,64]{0,1:T(8,128)S(1)} %fusion.18), kind=kOutput, calls=%fused_computation.7 | convolution fusion | flops 302002176 | bytes 2114304 | tf_op jit(solution)/shard_map/tci,tk,tr->kcri/dot_general | solution.py:45
  23.9 1.1 copy.43
  25.1 1.3 %collective-permute-start.3 = (f32[16,8192]{1,0:T(8,128)}, f32[16,8192]{1,0:T(8,128)}, u32[]{:S(2)}, u32[]{:S(2)}) collective-permute-start(f32[16,8192]{1,0:T(8,128)} %bitcast.93), channel_id=1, source_target_pairs={{4,0},{6,2},{8,4},{10,6},{12,8},{14,10},{16,12},{18,14},{20,16},{2... | collective-permute-start | bytes 1572872 | tf_op jit(solution)/shard_map/ppermute | solution.py:12
  26.3 1.1 copy.44
  27.5 1.3 %collective-permute-start.2 = (f32[16,8192]{1,0:T(8,128)}, f32[16,8192]{1,0:T(8,128)}, u32[]{:S(2)}, u32[]{:S(2)}) collective-permute-start(f32[16,8192]{1,0:T(8,128)} %bitcast.94), channel_id=1, source_target_pairs={{2,0},{4,2},{6,4},{8,6},{10,8},{12,10},{14,12},{16,14},{18,16},{20... | collective-permute-start | bytes 1572872 | tf_op jit(solution)/shard_map/ppermute | solution.py:12
  29.5 1.0 pad_maximum_fusion
  30.5 1.9 %gather_fusion.1 = bf16[64,16,128]{2,1,0:T(8,128)(2,1)S(1)} fusion(bf16[3,16,64,128]{3,1,2,0:T(8,128)(2,1)} %pad_maximum_fusion, s32[64]{0:T(128)S(1)} %fusion.36), kind=kCustom, calls=%fused_computation.1 | custom fusion | bytes 524800 | tf_op jit(solution)/shard_map/gather | solution.py:28
  32.4 1.2 fusion
  33.6 0.7 fusion.7
  34.3 6.7 %collective-permute-done.3 = f32[16,8192]{1,0:T(8,128)} collective-permute-done((f32[16,8192]{1,0:T(8,128)}, f32[16,8192]{1,0:T(8,128)}, u32[]{:S(2)}, u32[]{:S(2)}) %collective-permute-start.3) | collective-permute-done | bytes 524320 | tf_op jit(solution)/shard_map/ppermute | solution.py:12
  41.0 2.6 %fusion.5 = f32[16,8192]{1,0:T(8,128)} fusion(f32[16,8192]{1,0:T(8,128)} %collective-permute-done.3, f32[16,8192]{1,0:T(8,128)} %collective-permute-done.2, f32[2,8,64,128]{3,2,1,0:T(8,128)S(1)} %bitcast.97, f32[2,8,64,128]{3,2,1,0:T(8,128)S(1)} %bitcast.98), kind=kLoop, calls=%fused_computation.14 | loop fusion | flops 393216 | bytes 2621440 | tf_op jit(solution)/shard_map/add | solution.py:52
  44.1 22.2 %reduce-scatter.2.cloned.1.call-done = f32[8,8192]{1,0:T(8,128)} async-done(((f32[16,8192]{1,0:T(8,128)}), f32[8,8192]{1,0:T(8,128)}) %reduce-scatter.2.cloned.1.call-update) | async-done | bytes 262160 | tf_op jit(solution)/shard_map/reduce_scatter | solution.py:77
  66.3 1.4 %convolution_bitcast_fusion.1 = f32[16,8]{1,0:T(8,128)S(1)} fusion(bf16[16,8192]{1,0:T(8,128)(2,1)S(1)} %all_gather.3, f32[8,8192]{1,0:T(8,128)} %reduce-scatter.2.cloned.1.call-done, bf16[8,8192]{1,0:T(8,128)(2,1)S(1)} %copy-done.1, f32[8192]{0:T(1024)S(1)} %copy-done.2), kind=kOutput, calls=%fused_computation.8 | convolution fusion | flops 12779520 | bytes 688640 | tf_op jit(solution)/shard_map/dot_general | solution.py:82
  67.9 39.5 %all-reduce = (f32[16,16]{1,0:T(8,128)S(1)}, f32[16,16]{1,0:T(8,128)S(1)}) all-reduce(f32[16,16]{1,0:T(8,128)S(1)} %dynamic_update_slice.7, f32[16,16]{1,0:T(8,128)S(1)} %dynamic_update_slice.6), channel_id=1, replica_groups=mesh['blk'=16,'sub'=2] {'blk','sub'}, use_global_device_ids=true, to_apply=%region_4.5 | all-reduce | flops 512 | bytes 4096 | tf_op jit(solution)/shard_map/psum | solution.py:86
  107.5 1.5 %cholesky.15 = f32[16,16]{1,0:T(8,128)S(1)} custom-call(f32[16,16]{1,0:T(8,128)S(1)} %fusion.27), custom_call_target="Cholesky" | custom-call | tf_op jit(solution)/shard_map/jit(cholesky)/cholesky | solution.py:16
  109.6 0.6 fusion.22
  110.3 1.2 %custom-call.8 = f32[1,16,16]{1,2,0:T(8,128)S(1)} custom-call(f32[1,16,16]{2,1,0:T(8,128)S(1)} %fusion.22), custom_call_target="InvertDiagBlocksLowerTriangular" | custom-call | tf_op jit(solution)/shard_map/triangular_solve | solution.py:18
  111.9 1.9 %convolution_subtract_fusion = f32[8,8192]{1,0:T(8,128)} fusion(bf16[16,8192]{1,0:T(8,128)(2,1)S(1)} %all_gather.3, f32[8,8192]{1,0:T(8,128)} %reduce-scatter.2.cloned.1.call-done, bf16[8,8192]{1,0:T(8,128)(2,1)S(1)} %copy-done.1, f32[8192]{0:T(1024)S(1)} %copy-done.2, f32[16,16]{0,1:T(8,128)S(1)} %fusion.23, s32[]{:T(128)S(6)} %select_n.42), kind=kOutput, calls=%fused_computation.2 | convolution fusion | flops 12845056 | bytes 954372 | tf_op jit(solution)/shard_map/dot_general | solution.py:89
  (41 shorter events, 3.4 us)
Async XLA Ops:
  6.5 15.1 %copy-start = (bf16[1,64,128,128]{3,2,1,0:T(8,128)(2,1)S(1)}, bf16[1,64,128,128]{3,2,1,0:T(8,128)(2,1)}, u32[]{:S(2)}) copy-start(bf16[1,64,128,128]{3,2,1,0:T(8,128)(2,1)} %param.11) | copy-start | bytes 6291460
  6.5 15.8 %copy-start.4 = (s32[1,64]{1,0:T(1,128)S(1)}, s32[1,64]{1,0:T(1,128)}, u32[]{:S(2)}) copy-start(s32[1,64]{1,0:T(1,128)} %param.13) | copy-start | bytes 772
  6.5 59.7 %reduce-scatter.2.cloned.1.call-start = ((), (), s32[]{:S(2)}) async-start(), calls=%async_computation.1 | async-start | bytes 786432 | tf_op jit(solution)/shard_map/reduce_scatter | solution.py:77
  14.1 14.9 %collective-permute-start.1 = (bf16[16,8192]{1,0:T(8,128)(2,1)S(1)}, bf16[16,8192]{1,0:T(8,128)(2,1)S(1)}, u32[]{:S(2)}, u32[]{:S(2)}) collective-permute-start(bf16[16,8192]{1,0:T(8,128)(2,1)S(1)} %all_gather.3), channel_id=1, source_target_pairs={{0,4},{2,6},{4,8},{6,10},{8,12},{10,14},{12,16},{14,18},{16,20},{1... | collective-permute-start | bytes 786440 | tf_op jit(solution)/shard_map/ppermute | solution.py:12
  17.6 11.6 %collective-permute-start = (bf16[16,8192]{1,0:T(8,128)(2,1)S(1)}, bf16[16,8192]{1,0:T(8,128)(2,1)S(1)}, u32[]{:S(2)}, u32[]{:S(2)}) collective-permute-start(bf16[16,8192]{1,0:T(8,128)(2,1)S(1)} %all_gather.3), channel_id=1, source_target_pairs={{0,2},{2,4},{4,6},{6,8},{8,10},{10,12},{12,14},{14,16},{16,18},{18... | collective-permute-start | bytes 786440 | tf_op jit(solution)/shard_map/ppermute | solution.py:12
  23.9 5.1 %copy-start.5 = (s32[1,64]{1,0:T(1,128)S(1)}, s32[1,64]{1,0:T(1,128)}, u32[]{:S(2)}) copy-start(s32[1,64]{1,0:T(1,128)} %param.14) | copy-start | bytes 772
  25.1 16.0 %collective-permute-start.3 = (f32[16,8192]{1,0:T(8,128)}, f32[16,8192]{1,0:T(8,128)}, u32[]{:S(2)}, u32[]{:S(2)}) collective-permute-start(f32[16,8192]{1,0:T(8,128)} %bitcast.93), channel_id=1, source_target_pairs={{4,0},{6,2},{8,4},{10,6},{12,8},{14,10},{16,12},{18,14},{20,16},{2... | collective-permute-start | bytes 1572872 | tf_op jit(solution)/shard_map/ppermute | solution.py:12
  27.5 13.6 %collective-permute-start.2 = (f32[16,8192]{1,0:T(8,128)}, f32[16,8192]{1,0:T(8,128)}, u32[]{:S(2)}, u32[]{:S(2)}) collective-permute-start(f32[16,8192]{1,0:T(8,128)} %bitcast.94), channel_id=1, source_target_pairs={{2,0},{4,2},{6,4},{8,6},{10,8},{12,10},{14,12},{16,14},{18,16},{20... | collective-permute-start | bytes 1572872 | tf_op jit(solution)/shard_map/ppermute | solution.py:12
  30.5 3.1 %copy-start.3 = (s32[1,64]{1,0:T(1,128)S(1)}, s32[1,64]{1,0:T(1,128)}, u32[]{:S(2)}) copy-start(s32[1,64]{1,0:T(1,128)} %param.12) | copy-start | bytes 772
  33.6 10.1 %copy-start.1 = (bf16[8,8192]{1,0:T(8,128)(2,1)S(1)}, bf16[8,8192]{1,0:T(8,128)(2,1)}, u32[]{:S(2)}) copy-start(bf16[8,8192]{1,0:T(8,128)(2,1)} %param.9) | copy-start | bytes 393220
  33.6 32.7 %copy-start.2 = (f32[8192]{0:T(1024)S(1)}, f32[8192]{0:T(1024)}, u32[]{:S(2)}) copy-start(f32[8192]{0:T(1024)} %param.10) | copy-start | bytes 98308
Sparse Core Ops, SparseCore 0:
  43.8 22.4 reduce-scatter.1
where the time goes:
time: 121 us
  blocking collectives  47 us (39%)
  waiting for transfers between devices  28.9 us (24%)
  between operations  14.3 us (12%)
  other arithmetic  8.95 us (7%)
  matrix products  7.91 us (7%)
  starting transfers between devices  7.45 us (6%)
  local copies, waits for them, and re-layouts  6.14 us (5%)
    psum x1, blocking collectives, on_device(): gram, projected = lax.psum((gram_full, proj_full), ('blk', 'sub'))  39.5 us
    reduce_scatter x1, waiting for transfers between devices, on_device(): lax.psum_scatter(send_back(mirror), 'sub', scatter_dimension=0, tiled=True)  22.2 us
    all_gather x1, blocking collectives, on_device(): whole = lax.all_gather(vectors, 'sub', axis=0, tiled=True)  7.51 us
    ppermute x4, starting transfers between devices, from_behind(): lax.ppermute(value, axis, [(source, source + steps) for source in range(f...  7.45 us
    ppermute x4, waiting for transfers between devices, from_behind(): lax.ppermute(value, axis, [(source, source + steps) for source in range(f...  6.71 us
    add x1, other arithmetic, send_back(): gathered_sum = gathered_sum + from_behind(pieces[offset], 'blk', -offset)  2.61 us
  transfers between devices with their start and end apart: 5, of which 2 were waited for; matrix products, arithmetic and copies ran while one was open for 10% of the time, Pallas kernels for 0%

commit v1 on v0

--- a/solution.py
+++ b/solution.py
@@ -83,7 +83,7 @@
     empty = jnp.zeros((width, width), jnp.float32)
     gram_full = lax.dynamic_update_slice(empty, gram_part, (0, part_index * columns))
     proj_full = lax.dynamic_update_slice(empty, proj_part, (0, part_index * columns))
-    gram, projected = lax.psum((gram_full, proj_full), ("blk", "sub"))
+    gram, projected = lax.psum(lax.psum((gram_full, proj_full), "sub"), "blk")
     coefficients = ritz_coefficients(gram, projected)
     mine = lax.dynamic_slice_in_dim(coefficients, part_index * columns, columns, 1)
     return applied - jnp.dot(mine.T, own_wide, precision=highest)

time: 121 us -> 148 us (1.22)
  blocking collectives: 47 us -> 73.9 us
    psum x1 -> x2, blocking collectives: 39.5 us -> 66.4 us  [on_device(): gram, projected = lax.psum(lax.psum((gram_full, proj_full), 'sub'), 'blk')]
  transfers between devices with their start and end apart: 5 -> 5, of which waited for: 2 -> 2; matrix products, arithmetic and copies ran while one was open for 10% -> 8% of each run, Pallas kernels for 0% -> 0%
where the time goes in v1:
time: 148 us
  blocking collectives  73.9 us (50%)
  waiting for transfers between devices  28.9 us (20%)
  between operations  14.3 us (10%)
  other arithmetic  8.93 us (6%)
  matrix products  7.9 us (5%)
  starting transfers between devices  7.45 us (5%)
  local copies, waits for them, and re-layouts  6.15 us (4%)
    psum x2, blocking collectives, on_device(): gram, projected = lax.psum(lax.psum((gram_full, proj_full), 'sub'), 'blk')  66.4 us
    reduce_scatter x1, waiting for transfers between devices, on_device(): lax.psum_scatter(send_back(mirror), 'sub', scatter_dimension=0, tiled=True)  22.2 us
    all_gather x1, blocking collectives, on_device(): whole = lax.all_gather(vectors, 'sub', axis=0, tiled=True)  7.51 us
    ppermute x4, starting transfers between devices, from_behind(): lax.ppermute(value, axis, [(source, source + steps) for source in range(f...  7.45 us
    ppermute x4, waiting for transfers between devices, from_behind(): lax.ppermute(value, axis, [(source, source + steps) for source in range(f...  6.71 us
  transfers between devices with their start and end apart: 5, of which 2 were waited for; matrix products, arithmetic and copies ran while one was open for 8% of the time, Pallas kernels for 0%

profile of v1, /device:TPU:0, one launch (start us, length us, event | category | flops | bytes accessed | tf_op | source)
XLA Modules:
  0.0 147.6 jit_solution(7460387213883948146)
XLA Ops:
  6.5 7.5 %all_gather.3 = bf16[16,8192]{1,0:T(8,128)(2,1)S(1)} all-gather(bf16[8,8192]{1,0:T(8,128)(2,1)} %param.9), channel_id=1, replica_groups=mesh['blk'=16,'sub'=2] {'sub'}, dimensions={0}, use_global_device_ids=true | all-gather | bytes 393216 | tf_op jit(solution)/shard_map/all_gather | solution.py:65
  14.1 3.6 %collective-permute-start.1 = (bf16[16,8192]{1,0:T(8,128)(2,1)S(1)}, bf16[16,8192]{1,0:T(8,128)(2,1)S(1)}, u32[]{:S(2)}, u32[]{:S(2)}) collective-permute-start(bf16[16,8192]{1,0:T(8,128)(2,1)S(1)} %all_gather.3), channel_id=1, source_target_pairs={{0,4},{2,6},{4,8},{6,10},{8,12},{10,14},{12,16},{14,18},{16,20},{1... | collective-permute-start | bytes 786440 | tf_op jit(solution)/shard_map/ppermute | solution.py:12
  17.6 1.3 collective-permute-start
  19.0 0.7 fusion.30
  19.7 0.7 fusion.29
  21.6 0.7 fusion.2
  22.3 1.4 convolution_bitcast_fusion
  23.9 1.1 copy.43
  25.0 1.3 collective-permute-start.3
  26.3 1.1 copy.44
  27.5 1.3 collective-permute-start.2
  29.5 1.0 pad_maximum_fusion
  30.5 1.9 %gather_fusion.1 = bf16[64,16,128]{2,1,0:T(8,128)(2,1)S(1)} fusion(bf16[3,16,64,128]{3,1,2,0:T(8,128)(2,1)} %pad_maximum_fusion, s32[64]{0:T(128)S(1)} %fusion.36), kind=kCustom, calls=%fused_computation.1 | custom fusion | bytes 524800 | tf_op jit(solution)/shard_map/gather | solution.py:28
  32.4 1.2 fusion
  33.6 0.7 fusion.7
  34.3 6.7 %collective-permute-done.3 = f32[16,8192]{1,0:T(8,128)} collective-permute-done((f32[16,8192]{1,0:T(8,128)}, f32[16,8192]{1,0:T(8,128)}, u32[]{:S(2)}, u32[]{:S(2)}) %collective-permute-start.3) | collective-permute-done | bytes 524320 | tf_op jit(solution)/shard_map/ppermute | solution.py:12
  41.0 2.6 %fusion.5 = f32[16,8192]{1,0:T(8,128)} fusion(f32[16,8192]{1,0:T(8,128)} %collective-permute-done.3, f32[16,8192]{1,0:T(8,128)} %collective-permute-done.2, f32[2,8,64,128]{3,2,1,0:T(8,128)S(1)} %bitcast.97, f32[2,8,64,128]{3,2,1,0:T(8,128)S(1)} %bitcast.98), kind=kLoop, calls=%fused_computation.14 | loop fusion | flops 393216 | bytes 2621440 | tf_op jit(solution)/shard_map/add | solution.py:52
  44.0 22.2 %reduce-scatter.2.cloned.1.call-done = f32[8,8192]{1,0:T(8,128)} async-done(((f32[16,8192]{1,0:T(8,128)}), f32[8,8192]{1,0:T(8,128)}) %reduce-scatter.2.cloned.1.call-update) | async-done | bytes 262160 | tf_op jit(solution)/shard_map/reduce_scatter | solution.py:77
  66.3 1.4 convolution_bitcast_fusion.1
  67.9 7.0 %all-reduce.1 = (f32[16,16]{1,0:T(8,128)S(1)}, f32[16,16]{1,0:T(8,128)S(1)}) all-reduce(f32[16,16]{1,0:T(8,128)S(1)} %dynamic_update_slice.7, f32[16,16]{1,0:T(8,128)S(1)} %dynamic_update_slice.6), channel_id=1, replica_groups=mesh['blk'=16,'sub'=2] {'sub'}, use_global_device_ids=true, to_apply=%region_5.0 | all-reduce | flops 512 | bytes 4096 | tf_op jit(solution)/shard_map/psum | solution.py:86
  74.9 59.5 %all-reduce = (f32[16,16]{1,0:T(8,128)S(1)}, f32[16,16]{1,0:T(8,128)S(1)}) all-reduce(f32[16,16]{1,0:T(8,128)S(1)} %get-tuple-element.19, f32[16,16]{1,0:T(8,128)S(1)} %get-tuple-element.20), channel_id=1, replica_groups=mesh['blk'=16,'sub'=2] {'blk'}, use_global_device_ids=true, to_apply=%region_6.7 | all-reduce | flops 512 | bytes 4096 | tf_op jit(solution)/shard_map/psum | solution.py:86
  134.4 1.5 cholesky.15
  137.2 1.2 custom-call.8
  138.8 1.9 %convolution_subtract_fusion = f32[8,8192]{1,0:T(8,128)} fusion(bf16[16,8192]{1,0:T(8,128)(2,1)S(1)} %all_gather.3, f32[8,8192]{1,0:T(8,128)} %reduce-scatter.2.cloned.1.call-done, bf16[8,8192]{1,0:T(8,128)(2,1)S(1)} %copy-done.1, f32[8192]{0:T(1024)S(1)} %copy-done.2, f32[16,16]{0,1:T(8,128)S(1)} %fusion.23, s32[]{:T(128)S(6)} %select_n.42), kind=kOutput, calls=%fused_computation.2 | convolution fusion | flops 12845056 | bytes 954372 | tf_op jit(solution)/shard_map/dot_general | solution.py:89
  (42 shorter events, 4.0 us)
Async XLA Ops:
  6.5 15.1 %copy-start = (bf16[1,64,128,128]{3,2,1,0:T(8,128)(2,1)S(1)}, bf16[1,64,128,128]{3,2,1,0:T(8,128)(2,1)}, u32[]{:S(2)}) copy-start(bf16[1,64,128,128]{3,2,1,0:T(8,128)(2,1)} %param.11) | copy-start | bytes 6291460
  6.5 15.8 %copy-start.4 = (s32[1,64]{1,0:T(1,128)S(1)}, s32[1,64]{1,0:T(1,128)}, u32[]{:S(2)}) copy-start(s32[1,64]{1,0:T(1,128)} %param.13) | copy-start | bytes 772
  6.5 59.7 %reduce-scatter.2.cloned.1.call-start = ((), (), s32[]{:S(2)}) async-start(), calls=%async_computation.1 | async-start | bytes 786432 | tf_op jit(solution)/shard_map/reduce_scatter | solution.py:77
  14.1 15.0 %collective-permute-start.1 = (bf16[16,8192]{1,0:T(8,128)(2,1)S(1)}, bf16[16,8192]{1,0:T(8,128)(2,1)S(1)}, u32[]{:S(2)}, u32[]{:S(2)}) collective-permute-start(bf16[16,8192]{1,0:T(8,128)(2,1)S(1)} %all_gather.3), channel_id=1, source_target_pairs={{0,4},{2,6},{4,8},{6,10},{8,12},{10,14},{12,16},{14,18},{16,20},{1... | collective-permute-start | bytes 786440 | tf_op jit(solution)/shard_map/ppermute | solution.py:12
  17.6 11.6 %collective-permute-start = (bf16[16,8192]{1,0:T(8,128)(2,1)S(1)}, bf16[16,8192]{1,0:T(8,128)(2,1)S(1)}, u32[]{:S(2)}, u32[]{:S(2)}) collective-permute-start(bf16[16,8192]{1,0:T(8,128)(2,1)S(1)} %all_gather.3), channel_id=1, source_target_pairs={{0,2},{2,4},{4,6},{6,8},{8,10},{10,12},{12,14},{14,16},{16,18},{18... | collective-permute-start | bytes 786440 | tf_op jit(solution)/shard_map/ppermute | solution.py:12
  23.9 5.1 %copy-start.5 = (s32[1,64]{1,0:T(1,128)S(1)}, s32[1,64]{1,0:T(1,128)}, u32[]{:S(2)}) copy-start(s32[1,64]{1,0:T(1,128)} %param.14) | copy-start | bytes 772
  25.0 16.0 %collective-permute-start.3 = (f32[16,8192]{1,0:T(8,128)}, f32[16,8192]{1,0:T(8,128)}, u32[]{:S(2)}, u32[]{:S(2)}) collective-permute-start(f32[16,8192]{1,0:T(8,128)} %bitcast.93), channel_id=1, source_target_pairs={{4,0},{6,2},{8,4},{10,6},{12,8},{14,10},{16,12},{18,14},{20,16},{2... | collective-permute-start | bytes 1572872 | tf_op jit(solution)/shard_map/ppermute | solution.py:12
  27.5 13.6 %collective-permute-start.2 = (f32[16,8192]{1,0:T(8,128)}, f32[16,8192]{1,0:T(8,128)}, u32[]{:S(2)}, u32[]{:S(2)}) collective-permute-start(f32[16,8192]{1,0:T(8,128)} %bitcast.94), channel_id=1, source_target_pairs={{2,0},{4,2},{6,4},{8,6},{10,8},{12,10},{14,12},{16,14},{18,16},{20... | collective-permute-start | bytes 1572872 | tf_op jit(solution)/shard_map/ppermute | solution.py:12
  30.5 3.1 %copy-start.3 = (s32[1,64]{1,0:T(1,128)S(1)}, s32[1,64]{1,0:T(1,128)}, u32[]{:S(2)}) copy-start(s32[1,64]{1,0:T(1,128)} %param.12) | copy-start | bytes 772
  33.6 10.1 %copy-start.1 = (bf16[8,8192]{1,0:T(8,128)(2,1)S(1)}, bf16[8,8192]{1,0:T(8,128)(2,1)}, u32[]{:S(2)}) copy-start(bf16[8,8192]{1,0:T(8,128)(2,1)} %param.9) | copy-start | bytes 393220
  33.6 32.7 %copy-start.2 = (f32[8192]{0:T(1024)S(1)}, f32[8192]{0:T(1024)}, u32[]{:S(2)}) copy-start(f32[8192]{0:T(1024)} %param.10) | copy-start | bytes 98308
Sparse Core Ops, SparseCore 0:
  43.8 22.4 reduce-scatter.1
